TPU v7x, 512 devices: a whole 4x8x8 slice. The times are simulated.
512 devices in a mesh: rows: 64 (over y, x, core), dates: 8 (over z).
Axes of the slice: x: 4, y: 8, z: 8, core: 2. Of those that a mesh axis runs over, the one named last changes fastest.
Arguments:
- obs_mask: int32 [16, 512, 4096], P('dates', 'rows'), may hold values 0 or 1
- precision: float32 [16, 512, 4096], P('dates', 'rows'), may hold values from 0.5 to 4
- observed: float32 [16, 512, 4096], P('dates', 'rows')
- edge_class: int32 [2, 512, 4096], P(None, 'rows'), may hold values from 0 to 7
- temporal_weight: float32 [15], replicated, may hold values from 0.5 to 4
- inverse: bfloat16 [16, 16, 512, 4096], P(None, None, 'rows', 'dates'), as said below
Outputs:
- solution: float32 [16, 512, 4096], P('dates', 'rows')
- residual: float32 [16, 512, 4096], P('dates', 'rows')
Inputs may be any that keep to these rules, and one draw needn't show every extreme that they name: `inverse`: each pixel's matrix is symmetric with a diagonal larger than the sum of magnitudes of its row's other entries.
All inputs are finite; a program needn't handle non-finite values. No bound on the sum of `obs_mask` on one device may be relied on, other than what follows from the above.
Results may differ from a plain program's by a relative error of at most 0.0065.
Values sent between devices are 32-bit elements; how exact they have to be, the bound alone decides.
A program may use at most 64 MiB of HBM per device.

v0:
```python
import jax
import jax.numpy as jnp
from jax import lax
from jax.sharding import PartitionSpec as P

mass_term = 0.1


def shifted(value, axis, steps):
    count = lax.axis_size(axis)
    first, last = (max(0, -steps), min(count, count - steps))
    return lax.ppermute(value, axis, [(i, i + steps) for i in range(first, last)])


def apply_inverse(inverse, values):
    total = inverse[:, 0].astype(jnp.float32) * values[0][None]
    for source in range(1, values.shape[0]):
        total = total + inverse[:, source].astype(jnp.float32) * values[source][None]
    return total


def body(obs_mask, precision, observed, edge_class, temporal_weight, inverse):
    dates_here, rows_here, columns = observed.shape
    cols_here = inverse.shape[3]
    line_start = lax.axis_index("rows") * rows_here
    lines_total = rows_here * lax.axis_size("rows")
    col_start = lax.axis_index("dates") * cols_here
    weight = obs_mask.astype(jnp.float32) * precision
    both = jnp.stack([weight, weight * observed])
    both = lax.all_to_all(both, "dates", split_axis=3, concat_axis=1, tiled=True)
    weight, rhs = (both[0], both[1])
    classes = 0.25 * (edge_class.astype(jnp.float32) + 1.0)
    col_ids = lax.broadcasted_iota(jnp.int32, (rows_here, columns), 1)
    row_ids = lax.broadcasted_iota(jnp.int32, (rows_here, cols_here), 0) + line_start
    across_all = jnp.where(col_ids == columns - 1, 0.0, classes[0])
    across_ext = jnp.pad(across_all, ((0, 0), (1, 0)))
    across_prev = lax.dynamic_slice_in_dim(across_ext, col_start, cols_here, 1)
    across = lax.dynamic_slice_in_dim(across_all, col_start, cols_here, 1)
    downward = lax.dynamic_slice_in_dim(classes[1], col_start, cols_here, 1)
    downward = jnp.where(row_ids == lines_total - 1, 0.0, downward)
    downward_prev = jnp.concatenate([shifted(downward[-1:], "rows", 1), downward[:-1]], axis=0)
    zero_one = jnp.zeros((1,), jnp.float32)
    tau_up = jnp.concatenate([temporal_weight, zero_one])[:, None, None]
    tau_down = jnp.concatenate([zero_one, temporal_weight])[:, None, None]
    centre = (
        mass_term
        + weight
        + (across + across_prev + downward + downward_prev)[None]
        + (tau_up + tau_down)
    )

    def operator(field):
        above = jnp.concatenate([shifted(field[:, -1:], "rows", 1), field[:, :-1]], axis=1)
        below = jnp.concatenate([field[:, 1:], shifted(field[:, :1], "rows", -1)], axis=1)
        left = jnp.concatenate([shifted(field[:, :, -1:], "dates", 1), field[:, :, :-1]], axis=2)
        right = jnp.concatenate([field[:, :, 1:], shifted(field[:, :, :1], "dates", -1)], axis=2)
        before = jnp.pad(field, ((1, 0), (0, 0), (0, 0)))[:-1]
        after = jnp.pad(field, ((0, 1), (0, 0), (0, 0)))[1:]
        return (
            centre * field
            - (across * right + across_prev * left)
            - (downward * below + downward_prev * above)
            - (tau_up * after + tau_down * before)
        )

    precond = apply_inverse(inverse, rhs)
    image = operator(precond)
    mapped = apply_inverse(inverse, image)
    mapped_image = operator(mapped)
    sums = jnp.stack(
        [
            jnp.sum(rhs * precond),
            jnp.sum(precond * image),
            jnp.sum(image * mapped),
            jnp.sum(mapped * mapped_image),
        ]
    )
    sums = lax.psum(sums, ("rows", "dates"))
    rz, dd, ee, ff = (sums[0], sums[1], sums[2], sums[3])
    alpha = rz / dd
    grown = alpha * ee / dd
    alpha_next = (alpha * alpha * ee - rz) / (alpha * alpha * (ff - ee * ee / dd))
    first = alpha + alpha_next * grown
    second = alpha_next * alpha
    out = jnp.stack(
        [first * precond - second * mapped, rhs - first * image + second * mapped_image]
    )
    out = lax.all_to_all(out, "dates", split_axis=1, concat_axis=3, tiled=True)
    return (out[0], out[1])


def solution(mesh):
    return jax.shard_map(
        body,
        mesh=mesh,
        in_specs=(
            P("dates", "rows", None),
            P("dates", "rows", None),
            P("dates", "rows", None),
            P(None, "rows", None),
            P(),
            P(None, None, "rows", "dates"),
        ),
        out_specs=(P("dates", "rows", None), P("dates", "rows", None)),
        check_vma=False,
    )
```

profile of v0, /device:TPU:26, one launch (start us, length us, event | category | flops | bytes accessed | tf_op | source)
XLA Modules:
  0.0 248.5 jit_solution(16082085440796772396)
XLA Ops:
  0.6 1.2 fusion.82
  1.8 8.2 %copy.156 = f32[2,2,8,4096]{2,1,0,3:T(2,128)} copy(f32[2,2,8,4096]{3,2,1,0:T(8,128)S(1)} %pad_maximum_fusion) | data formatting | bytes 1048576 | tf_op jit(solution)/shard_map/stack | solution.py:29
  10.0 15.6 %reshape.805 = f32[8,1,16384]{2,1,0:T(1,128)} reshape(f32[4096,2,2,8]{3,2,1,0:T(2,128)} %bitcast.617) | data formatting | bytes 1048576
  25.7 10.4 %all-to-all-start = ((f32[8,1,16384]{2,1,0:T(1,128)}), f32[8,1,16384]{2,1,0:T(1,128)S(1)}, u32[]{:S(2)}, u32[]{:S(2)}) async-start(f32[8,1,16384]{2,1,0:T(1,128)} %reshape.805), calls=%async_computation | async-start | bytes 1048576 | tf_op jit(solution)/shard_map/all_to_all | solution.py:30
  36.1 0.0 copy-done.23
  36.2 0.1 bitcast_select_fusion
  36.3 2.1 collective-permute-start
  38.4 0.7 select_bitcast_fusion
  39.1 0.0 copy-done
  39.1 1.9 bitcast_convert_fusion.15
  41.0 0.0 copy-done.32
  41.0 0.7 fusion.83
  41.7 0.0 collective-permute-done
  41.7 0.7 add_add_fusion
  42.4 11.2 %all-to-all-done = f32[8,1,16384]{2,1,0:T(1,128)S(1)} async-done(((f32[8,1,16384]{2,1,0:T(1,128)}), f32[8,1,16384]{2,1,0:T(1,128)S(1)}, u32[]{:S(2)}, u32[]{:S(2)}) %all-to-all-start) | async-done | bytes 524320 | tf_op jit(solution)/shard_map/all_to_all | solution.py:30
  53.6 0.5 broadcast.381
  54.1 1.9 reduce.1
  56.0 16.0 %reshape.806 = f32[4096,2,2,8]{3,2,1,0:T(2,128)} reshape(f32[8,16384]{1,0:T(8,128)S(1)} %reduce.1) | data formatting | bytes 1048576
  72.0 10.1 %copy.158 = f32[2,2,8,8,512]{4,2,1,3,0:T(8,128)S(1)} copy(f32[2,2,8,8,512]{2,1,0,4,3:T(2,128)} %bitcast.618) | data formatting | bytes 1048576 | tf_op jit(solution)/shard_map/all_to_all | solution.py:30
  82.2 0.0 copy-start.16
  82.2 0.0 copy-start.17
  82.2 0.0 copy-start.18
  82.3 0.0 copy-start.1
  82.3 0.0 copy-start.2
  82.5 0.4 fusion.51
  82.9 0.1 fusion.91
  82.9 0.1 fusion.92
  83.1 1.4 collective-permute-start.1
  84.5 4.5 %collective-permute-start.2 = (f32[16,8,1]{2,1,0:T(8,128)S(1)}, f32[16,8,1]{2,1,0:T(8,128)S(1)}, u32[]{:S(2)}, u32[]{:S(2)}) collective-permute-start(f32[16,8,1]{2,1,0:T(8,128)S(1)} %get-tuple-element.60), channel_id=1, source_target_pairs={{0,1},{1,2},{2,3},{3,4},{4,5},{5,6},{6,7},{8,9},{9,10},{10,11},{11... | collective-permute-start | bytes 1544 | tf_op jit(solution)/shard_map/ppermute | solution.py:12
  89.1 1.9 collective-permute-start.3
  91.0 2.4 collective-permute-start.4
  93.6 1.2 multiply_reduce_fusion.3
  94.9 0.1 fusion.93
  95.0 0.0 collective-permute-done.1
  95.0 0.0 collective-permute-done.2
  95.0 0.0 collective-permute-done.3
  95.0 1.2 collective-permute-done.4
  96.2 0.0 copy-done.25
  96.3 0.3 fusion.2
  96.6 0.4 fusion.52
  97.1 0.1 fusion.86
  97.2 0.1 fusion.87
  97.3 1.3 collective-permute-start.5
  98.6 4.5 %collective-permute-start.6 = (f32[16,8,1]{2,1,0:T(8,128)S(1)}, f32[16,8,1]{2,1,0:T(8,128)S(1)}, u32[]{:S(2)}, u32[]{:S(2)}) collective-permute-start(f32[16,8,1]{2,1,0:T(8,128)S(1)} %get-tuple-element.35), channel_id=1, source_target_pairs={{0,1},{1,2},{2,3},{3,4},{4,5},{5,6},{6,7},{8,9},{9,10},{10,11},{11... | collective-permute-start | bytes 1544 | tf_op jit(solution)/shard_map/ppermute | solution.py:12
  103.2 1.9 collective-permute-start.7
  105.1 2.6 %collective-permute-start.8 = (f32[16,1,512]{2,1,0:T(1,128)S(1)}, f32[16,1,512]{2,1,0:T(1,128)S(1)}, u32[]{:S(2)}, u32[]{:S(2)}) collective-permute-start(f32[16,1,512]{2,1,0:T(1,128)S(1)} %get-tuple-element.39), channel_id=1, source_target_pairs={{0,8},{8,16},{16,24},{24,32},{32,40},{40,48},{48,56},{56,64},{64,7... | collective-permute-start | bytes 98312 | tf_op jit(solution)/shard_map/ppermute | solution.py:12
  107.7 0.1 fusion.88
  107.8 0.0 collective-permute-done.5
  107.8 0.0 collective-permute-done.6
  107.8 0.0 collective-permute-done.7
  107.8 5.2 %collective-permute-done.8 = f32[16,1,512]{2,1,0:T(1,128)S(1)} collective-permute-done((f32[16,1,512]{2,1,0:T(1,128)S(1)}, f32[16,1,512]{2,1,0:T(1,128)S(1)}, u32[]{:S(2)}, u32[]{:S(2)}) %collective-permute-start.8) | collective-permute-done | bytes 32800 | tf_op jit(solution)/shard_map/ppermute | solution.py:12
  113.1 0.0 copy-done.19
  113.1 0.0 copy-done.20
  113.1 0.0 copy-done.21
  113.1 0.0 copy-done.22
  113.1 1.5 multiply_reduce_fusion.2
  114.6 2.6 %pad_maximum_fusion.5 = f32[4]{0:T(128)S(1)} fusion(f32[1]{0:T(128)} %bitcast.76, f32[1]{0:T(128)} %bitcast.75, f32[1]{0:T(128)} %bitcast.58, f32[1]{0:T(128)} %bitcast.37), kind=kLoop, calls=%fused_computation.229 | loop fusion | flops 12 | bytes 32 | tf_op jit(solution)/shard_map/stack | solution.py:70
  117.2 100.8 %psum.7 = f32[4]{0:T(128)S(1)} all-reduce(f32[4]{0:T(128)S(1)} %pad_maximum_fusion.5), channel_id=1, replica_groups=mesh['rows'=64,'dates'=8] {'rows','dates'}, use_global_device_ids=true, to_apply=%region_4.5 | all-reduce | flops 4 | bytes 32 | tf_op jit(solution)/shard_map/psum | solution.py:78
  218.0 0.6 fusion.94
  225.1 1.6 fusion.19
  226.7 0.1 add_bitcast_fusion
  226.8 20.2 %all_to_all.30 = f32[2,16,8,512]{3,2,0,1:T(8,128)S(1)} all-to-all(f32[2,16,8,512]{3,2,0,1:T(8,128)S(1)} %pad_maximum_fusion.1), channel_id=1, replica_groups=mesh['rows'=64,'dates'=8] {'dates'}, dimensions={1} | all-to-all | bytes 1048576 | tf_op jit(solution)/shard_map/all_to_all | solution.py:88
  247.0 0.7 copy.176
  247.8 0.7 copy.177
  (67 shorter events, 0.5 us)
Async XLA Ops:
  10.0 26.1 %copy-start.23 = (s32[2,8,4096]{2,1,0:T(8,128)S(1)}, s32[2,8,4096]{2,1,0:T(8,128)}, u32[]{:S(2)}) copy-start(s32[2,8,4096]{2,1,0:T(8,128)} %param.9) | copy-start | bytes 786436
  25.7 13.4 %copy-start = (bf16[16,16,8,512]{3,2,1,0:T(8,128)(2,1)S(1)}, bf16[16,16,8,512]{3,2,1,0:T(8,128)(2,1)}, u32[]{:S(2)}) copy-start(bf16[16,16,8,512]{3,2,1,0:T(8,128)(2,1)} %param.11) | copy-start | bytes 6291460
  25.7 27.9 %all-to-all-start = ((f32[8,1,16384]{2,1,0:T(1,128)}), f32[8,1,16384]{2,1,0:T(1,128)S(1)}, u32[]{:S(2)}, u32[]{:S(2)}) async-start(f32[8,1,16384]{2,1,0:T(1,128)} %reshape.805), calls=%async_computation | async-start | bytes 1048576 | tf_op jit(solution)/shard_map/all_to_all | solution.py:30
  36.3 5.4 %collective-permute-start = (f32[1,512]{1,0:T(1,128)S(1)}, f32[1,512]{1,0:T(1,128)S(1)}, u32[]{:S(2)}, u32[]{:S(2)}) collective-permute-start(f32[1,512]{1,0:T(1,128)S(1)} %slice.360), channel_id=1, source_target_pairs={{0,8},{8,16},{16,24},{24,32},{32,40},{40,48},{48,56},{56,64},{64,7... | collective-permute-start | bytes 6152 | tf_op jit(solution)/shard_map/ppermute | solution.py:12
  39.1 1.9 copy-start.32
  82.2 30.8 %copy-start.16 = (f32[8,512]{1,0:T(8,128)}, f32[8,512]{1,0:T(8,128)S(1)}, u32[]{:S(2)}) copy-start(f32[8,512]{1,0:T(8,128)S(1)} %get-tuple-element.73) | copy-start | bytes 49156
  82.2 30.8 %copy-start.17 = (f32[8,512]{1,0:T(8,128)}, f32[8,512]{1,0:T(8,128)S(1)}, u32[]{:S(2)}) copy-start(f32[8,512]{1,0:T(8,128)S(1)} %get-tuple-element.74) | copy-start | bytes 49156
  82.2 30.8 %copy-start.18 = (f32[8,512]{1,0:T(8,128)}, f32[8,512]{1,0:T(8,128)S(1)}, u32[]{:S(2)}) copy-start(f32[8,512]{1,0:T(8,128)S(1)} %get-tuple-element.75) | copy-start | bytes 49156
  82.3 30.8 %copy-start.19 = (f32[8,512]{1,0:T(8,128)}, f32[8,512]{1,0:T(8,128)S(1)}, u32[]{:S(2)}) copy-start(f32[8,512]{1,0:T(8,128)S(1)} %get-tuple-element.76) | copy-start | bytes 49156
  82.3 30.8 %copy-start.20 = (f32[8,512]{1,0:T(8,128)}, f32[8,512]{1,0:T(8,128)S(1)}, u32[]{:S(2)}) copy-start(f32[8,512]{1,0:T(8,128)S(1)} %get-tuple-element.77) | copy-start | bytes 49156
  82.3 30.8 %copy-start.21 = (f32[8,512]{1,0:T(8,128)}, f32[8,512]{1,0:T(8,128)S(1)}, u32[]{:S(2)}) copy-start(f32[8,512]{1,0:T(8,128)S(1)} %get-tuple-element.78) | copy-start | bytes 49156
  82.3 30.8 %copy-start.22 = (f32[8,512]{1,0:T(8,128)}, f32[8,512]{1,0:T(8,128)S(1)}, u32[]{:S(2)}) copy-start(f32[8,512]{1,0:T(8,128)S(1)} %get-tuple-element.79) | copy-start | bytes 49156
  82.3 11.1 %copy-start.1 = (f32[16,1,8,512]{3,2,0,1:T(8,128)S(1)}, f32[16,1,8,512]{3,2,0,1:T(8,128)}, u32[]{:S(2)}) copy-start(f32[16,1,8,512]{3,2,0,1:T(8,128)} %get-tuple-element.11) | copy-start | bytes 786436
  82.3 11.1 %copy-start.2 = (f32[16,1,8,512]{3,2,0,1:T(8,128)S(1)}, f32[16,1,8,512]{3,2,0,1:T(8,128)}, u32[]{:S(2)}) copy-start(f32[16,1,8,512]{3,2,0,1:T(8,128)} %get-tuple-element.12) | copy-start | bytes 786436
  82.3 11.1 %copy-start.3 = (f32[16,1,8,512]{3,2,0,1:T(8,128)S(1)}, f32[16,1,8,512]{3,2,0,1:T(8,128)}, u32[]{:S(2)}) copy-start(f32[16,1,8,512]{3,2,0,1:T(8,128)} %get-tuple-element.13) | copy-start | bytes 786436
  82.3 11.1 %copy-start.4 = (f32[16,1,8,512]{3,2,0,1:T(8,128)S(1)}, f32[16,1,8,512]{3,2,0,1:T(8,128)}, u32[]{:S(2)}) copy-start(f32[16,1,8,512]{3,2,0,1:T(8,128)} %get-tuple-element.14) | copy-start | bytes 786436
  82.3 11.1 %copy-start.5 = (f32[16,1,8,512]{3,2,0,1:T(8,128)S(1)}, f32[16,1,8,512]{3,2,0,1:T(8,128)}, u32[]{:S(2)}) copy-start(f32[16,1,8,512]{3,2,0,1:T(8,128)} %get-tuple-element.15) | copy-start | bytes 786436
  82.4 11.1 %copy-start.6 = (f32[16,1,8,512]{3,2,0,1:T(8,128)S(1)}, f32[16,1,8,512]{3,2,0,1:T(8,128)}, u32[]{:S(2)}) copy-start(f32[16,1,8,512]{3,2,0,1:T(8,128)} %get-tuple-element.16) | copy-start | bytes 786436
  82.4 11.1 %copy-start.7 = (f32[16,1,8,512]{3,2,0,1:T(8,128)S(1)}, f32[16,1,8,512]{3,2,0,1:T(8,128)}, u32[]{:S(2)}) copy-start(f32[16,1,8,512]{3,2,0,1:T(8,128)} %get-tuple-element.17) | copy-start | bytes 786436
  82.4 11.1 %copy-start.8 = (f32[16,1,8,512]{3,2,0,1:T(8,128)S(1)}, f32[16,1,8,512]{3,2,0,1:T(8,128)}, u32[]{:S(2)}) copy-start(f32[16,1,8,512]{3,2,0,1:T(8,128)} %get-tuple-element.18) | copy-start | bytes 786436
  82.4 11.1 %copy-start.9 = (f32[16,1,8,512]{3,2,0,1:T(8,128)S(1)}, f32[16,1,8,512]{3,2,0,1:T(8,128)}, u32[]{:S(2)}) copy-start(f32[16,1,8,512]{3,2,0,1:T(8,128)} %get-tuple-element.19) | copy-start | bytes 786436
  82.4 11.1 %copy-start.10 = (f32[16,1,8,512]{3,2,0,1:T(8,128)S(1)}, f32[16,1,8,512]{3,2,0,1:T(8,128)}, u32[]{:S(2)}) copy-start(f32[16,1,8,512]{3,2,0,1:T(8,128)} %get-tuple-element.20) | copy-start | bytes 786436
  82.4 11.1 %copy-start.11 = (f32[16,1,8,512]{3,2,0,1:T(8,128)S(1)}, f32[16,1,8,512]{3,2,0,1:T(8,128)}, u32[]{:S(2)}) copy-start(f32[16,1,8,512]{3,2,0,1:T(8,128)} %get-tuple-element.21) | copy-start | bytes 786436
  82.4 11.1 %copy-start.12 = (f32[16,1,8,512]{3,2,0,1:T(8,128)S(1)}, f32[16,1,8,512]{3,2,0,1:T(8,128)}, u32[]{:S(2)}) copy-start(f32[16,1,8,512]{3,2,0,1:T(8,128)} %get-tuple-element.22) | copy-start | bytes 786436
  82.4 11.1 %copy-start.13 = (f32[16,1,8,512]{3,2,0,1:T(8,128)S(1)}, f32[16,1,8,512]{3,2,0,1:T(8,128)}, u32[]{:S(2)}) copy-start(f32[16,1,8,512]{3,2,0,1:T(8,128)} %get-tuple-element.23) | copy-start | bytes 786436
  82.4 11.1 %copy-start.14 = (f32[16,1,8,512]{3,2,0,1:T(8,128)S(1)}, f32[16,1,8,512]{3,2,0,1:T(8,128)}, u32[]{:S(2)}) copy-start(f32[16,1,8,512]{3,2,0,1:T(8,128)} %get-tuple-element.24) | copy-start | bytes 786436
  82.4 11.1 %copy-start.15 = (f32[16,1,8,512]{3,2,0,1:T(8,128)S(1)}, f32[16,1,8,512]{3,2,0,1:T(8,128)}, u32[]{:S(2)}) copy-start(f32[16,1,8,512]{3,2,0,1:T(8,128)} %get-tuple-element.25) | copy-start | bytes 786436
  83.1 11.9 %collective-permute-start.1 = (f32[16,8,1]{2,1,0:T(8,128)S(1)}, f32[16,8,1]{2,1,0:T(8,128)S(1)}, u32[]{:S(2)}, u32[]{:S(2)}) collective-permute-start(f32[16,8,1]{2,1,0:T(8,128)S(1)} %get-tuple-element.61), channel_id=1, source_target_pairs={{1,0},{2,1},{3,2},{4,3},{5,4},{6,5},{7,6},{9,8},{10,9},{11,10},{12... | collective-permute-start | bytes 1544 | tf_op jit(solution)/shard_map/ppermute | solution.py:12
  84.5 10.5 %collective-permute-start.2 = (f32[16,8,1]{2,1,0:T(8,128)S(1)}, f32[16,8,1]{2,1,0:T(8,128)S(1)}, u32[]{:S(2)}, u32[]{:S(2)}) collective-permute-start(f32[16,8,1]{2,1,0:T(8,128)S(1)} %get-tuple-element.60), channel_id=1, source_target_pairs={{0,1},{1,2},{2,3},{3,4},{4,5},{5,6},{6,7},{8,9},{9,10},{10,11},{11... | collective-permute-start | bytes 1544 | tf_op jit(solution)/shard_map/ppermute | solution.py:12
  89.1 6.0 %collective-permute-start.3 = (f32[16,1,512]{2,1,0:T(1,128)S(1)}, f32[16,1,512]{2,1,0:T(1,128)S(1)}, u32[]{:S(2)}, u32[]{:S(2)}) collective-permute-start(f32[16,1,512]{2,1,0:T(1,128)S(1)} %get-tuple-element.57), channel_id=1, source_target_pairs={{8,0},{16,8},{24,16},{32,24},{40,32},{48,40},{56,48},{64,56},{72,6... | collective-permute-start | bytes 98312 | tf_op jit(solution)/shard_map/ppermute | solution.py:12
  91.0 5.2 %collective-permute-start.4 = (f32[16,1,512]{2,1,0:T(1,128)S(1)}, f32[16,1,512]{2,1,0:T(1,128)S(1)}, u32[]{:S(2)}, u32[]{:S(2)}) collective-permute-start(f32[16,1,512]{2,1,0:T(1,128)S(1)} %get-tuple-element.56), channel_id=1, source_target_pairs={{0,8},{8,16},{16,24},{24,32},{32,40},{40,48},{48,56},{56,64},{64,7... | collective-permute-start | bytes 98312 | tf_op jit(solution)/shard_map/ppermute | solution.py:12
  93.5 2.7 %copy-start.24 = (f32[8,512]{1,0:T(8,128)S(1)}, f32[8,512]{1,0:T(8,128)}, u32[]{:S(2)}) copy-start(f32[8,512]{1,0:T(8,128)} %select_bitcast_fusion) | copy-start | bytes 49156
  93.6 2.7 %copy-start.25 = (f32[8,512]{1,0:T(8,128)S(1)}, f32[8,512]{1,0:T(8,128)}, u32[]{:S(2)}) copy-start(f32[8,512]{1,0:T(8,128)} %get-tuple-element.6) | copy-start | bytes 49156
  93.6 2.7 %copy-start.26 = (f32[8,512]{1,0:T(8,128)S(1)}, f32[8,512]{1,0:T(8,128)}, u32[]{:S(2)}) copy-start(f32[8,512]{1,0:T(8,128)} %get-tuple-element.7) | copy-start | bytes 49156
  93.6 2.7 %copy-start.27 = (f32[8,512]{1,0:T(8,128)S(1)}, f32[8,512]{1,0:T(8,128)}, u32[]{:S(2)}) copy-start(f32[8,512]{1,0:T(8,128)} %get-tuple-element.8) | copy-start | bytes 49156
  93.6 2.7 %copy-start.28 = (f32[8,512]{1,0:T(8,128)S(1)}, f32[8,512]{1,0:T(8,128)}, u32[]{:S(2)}) copy-start(f32[8,512]{1,0:T(8,128)} %get-tuple-element.9) | copy-start | bytes 49156
  93.6 2.7 %copy-start.29 = (f32[16]{0:T(128)S(1)}, f32[16]{0:T(128)}, u32[]{:S(2)}) copy-start(f32[16]{0:T(128)} %get-tuple-element.84) | copy-start | bytes 196
  93.6 2.7 %copy-start.30 = (f32[16]{0:T(128)S(1)}, f32[16]{0:T(128)}, u32[]{:S(2)}) copy-start(f32[16]{0:T(128)} %get-tuple-element.85) | copy-start | bytes 196
  93.6 2.7 %copy-start.31 = (f32[16]{0:T(128)S(1)}, f32[16]{0:T(128)}, u32[]{:S(2)}) copy-start(f32[16]{0:T(128)} %get-tuple-element.86) | copy-start | bytes 196
  97.3 10.5 %collective-permute-start.5 = (f32[16,8,1]{2,1,0:T(8,128)S(1)}, f32[16,8,1]{2,1,0:T(8,128)S(1)}, u32[]{:S(2)}, u32[]{:S(2)}) collective-permute-start(f32[16,8,1]{2,1,0:T(8,128)S(1)} %get-tuple-element.34), channel_id=1, source_target_pairs={{1,0},{2,1},{3,2},{4,3},{5,4},{6,5},{7,6},{9,8},{10,9},{11,10},{12... | collective-permute-start | bytes 1544 | tf_op jit(solution)/shard_map/ppermute | solution.py:12
  98.6 9.2 %collective-permute-start.6 = (f32[16,8,1]{2,1,0:T(8,128)S(1)}, f32[16,8,1]{2,1,0:T(8,128)S(1)}, u32[]{:S(2)}, u32[]{:S(2)}) collective-permute-start(f32[16,8,1]{2,1,0:T(8,128)S(1)} %get-tuple-element.35), channel_id=1, source_target_pairs={{0,1},{1,2},{2,3},{3,4},{4,5},{5,6},{6,7},{8,9},{9,10},{10,11},{11... | collective-permute-start | bytes 1544 | tf_op jit(solution)/shard_map/ppermute | solution.py:12
  103.2 4.6 %collective-permute-start.7 = (f32[16,1,512]{2,1,0:T(1,128)S(1)}, f32[16,1,512]{2,1,0:T(1,128)S(1)}, u32[]{:S(2)}, u32[]{:S(2)}) collective-permute-start(f32[16,1,512]{2,1,0:T(1,128)S(1)} %get-tuple-element.38), channel_id=1, source_target_pairs={{8,0},{16,8},{24,16},{32,24},{40,32},{48,40},{56,48},{64,56},{72,6... | collective-permute-start | bytes 98312 | tf_op jit(solution)/shard_map/ppermute | solution.py:12
  105.1 7.9 %collective-permute-start.8 = (f32[16,1,512]{2,1,0:T(1,128)S(1)}, f32[16,1,512]{2,1,0:T(1,128)S(1)}, u32[]{:S(2)}, u32[]{:S(2)}) collective-permute-start(f32[16,1,512]{2,1,0:T(1,128)S(1)} %get-tuple-element.39), channel_id=1, source_target_pairs={{0,8},{8,16},{16,24},{24,32},{32,40},{40,48},{48,56},{56,64},{64,7... | collective-permute-start | bytes 98312 | tf_op jit(solution)/shard_map/ppermute | solution.py:12
where the time goes:
time: 249 us; the launch traced here: 248 us
  blocking collectives  121 us (49%)
  local copies, waits for them, and re-layouts  53.4 us (21%)
  starting transfers between devices  33.2 us (13%)
  waiting for transfers between devices  17.6 us (7%)
  other arithmetic  15.4 us (6%)
  between operations  7.91 us (3%)
    psum x1, blocking collectives, body(): sums = lax.psum(sums, ('rows', 'dates'))  101 us
    unnamed x68, local copies, waits for them, and re-layouts  31.8 us
    ppermute x9, starting transfers between devices, shifted(): lax.ppermute(value, axis, [(i, i + steps) for i in range(first, last)])  22.8 us
    all_to_all x1, blocking collectives, body(): out = lax.all_to_all(out, 'dates', split_axis=1, concat_axis=3, tiled=True)  20.2 us
    all_to_all x1, waiting for transfers between devices, body(): lax.all_to_all(both, 'dates', split_axis=3, concat_axis=1, tiled=True)  11.2 us
    all_to_all x2, local copies, waits for them, and re-layouts, body(): lax.all_to_all(both, 'dates', split_axis=3, concat_axis=1, tiled=True)  10.6 us
    all_to_all x1, starting transfers between devices, body(): lax.all_to_all(both, 'dates', split_axis=3, concat_axis=1, tiled=True)  10.4 us
    another operation x1, local copies, waits for them, and re-layouts, body(): both = jnp.stack([weight, weight * observed])  8.2 us
  transfers between devices with their start and end apart: 10, of which 3 were waited for; matrix products, arithmetic and copies ran while one was open for 2% of the time, Pallas kernels for 0%

commit v1 on v0

--- a/solution.py
+++ b/solution.py
@@ -4,6 +4,12 @@
 from jax.sharding import PartitionSpec as P
 
 mass_term = 0.1
+
+
+def treat_joints(net_axis, x_part, named_axis):
+    for num in (net_axis, named_axis):
+        x_part = lax.psum(x_part, axis_name=num)
+    return x_part
 
 
 def shifted(value, axis, steps):
@@ -75,7 +81,7 @@
             jnp.sum(mapped * mapped_image),
         ]
     )
-    sums = lax.psum(sums, ("rows", "dates"))
+    sums = treat_joints("dates", sums, "rows")
     rz, dd, ee, ff = (sums[0], sums[1], sums[2], sums[3])
     alpha = rz / dd
     grown = alpha * ee / dd

time: 249 us -> 294 us (1.18)
  the two profiles are of different devices: /device:TPU:26 before, /device:TPU:32 now
where the time goes in v1:
time: 294 us; the launch traced here: 293 us
  blocking collectives  160 us (54%)
  local copies, waits for them, and re-layouts  53.4 us (18%)
  starting transfers between devices  34.4 us (12%)
  waiting for transfers between devices  22.1 us (8%)
  other arithmetic  15.2 us (5%)
  between operations  7.68 us (3%)
    psum x2, blocking collectives, treat_joints(): x_part = lax.psum(x_part, axis_name=num)  138 us
    unnamed x68, local copies, waits for them, and re-layouts  31.8 us
    ppermute x9, starting transfers between devices, shifted(): lax.ppermute(value, axis, [(i, i + steps) for i in range(first, last)])  24 us
    all_to_all x1, blocking collectives, body(): out = lax.all_to_all(out, 'dates', split_axis=1, concat_axis=3, tiled=True)  21.6 us
    ppermute x9, waiting for transfers between devices, shifted(): lax.ppermute(value, axis, [(i, i + steps) for i in range(first, last)])  13.7 us
    all_to_all x2, local copies, waits for them, and re-layouts, body(): lax.all_to_all(both, 'dates', split_axis=3, concat_axis=1, tiled=True)  10.6 us
    all_to_all x1, starting transfers between devices, body(): lax.all_to_all(both, 'dates', split_axis=3, concat_axis=1, tiled=True)  10.4 us
    all_to_all x1, waiting for transfers between devices, body(): lax.all_to_all(both, 'dates', split_axis=3, concat_axis=1, tiled=True)  8.42 us
  transfers between devices with their start and end apart: 10, of which 4 were waited for; matrix products, arithmetic and copies ran while one was open for 2% of the time, Pallas kernels for 0%

profile of v1, /device:TPU:32, one launch (start us, length us, event | category | flops | bytes accessed | tf_op | source)
XLA Modules:
  0.0 292.9 jit_solution(13214234882895071796)
XLA Ops:
  0.6 1.2 fusion.82
  1.8 8.2 %copy.156 = f32[2,2,8,4096]{2,1,0,3:T(2,128)} copy(f32[2,2,8,4096]{3,2,1,0:T(8,128)S(1)} %pad_maximum_fusion) | data formatting | bytes 1048576 | tf_op jit(solution)/shard_map/stack | solution.py:35
  10.0 15.6 %reshape.805 = f32[8,1,16384]{2,1,0:T(1,128)} reshape(f32[4096,2,2,8]{3,2,1,0:T(2,128)} %bitcast.617) | data formatting | bytes 1048576
  25.7 10.4 %all-to-all-start = ((f32[8,1,16384]{2,1,0:T(1,128)}), f32[8,1,16384]{2,1,0:T(1,128)S(1)}, u32[]{:S(2)}, u32[]{:S(2)}) async-start(f32[8,1,16384]{2,1,0:T(1,128)} %reshape.805), calls=%async_computation | async-start | bytes 1048576 | tf_op jit(solution)/shard_map/all_to_all | solution.py:36
  36.1 0.0 copy-done.23
  36.2 0.1 bitcast_select_fusion
  36.3 2.1 collective-permute-start
  38.4 0.7 select_bitcast_fusion
  39.1 1.9 bitcast_convert_fusion.15
  41.0 0.6 fusion.83
  41.7 2.8 collective-permute-done
  44.5 0.7 add_add_fusion
  45.2 8.4 %all-to-all-done = f32[8,1,16384]{2,1,0:T(1,128)S(1)} async-done(((f32[8,1,16384]{2,1,0:T(1,128)}), f32[8,1,16384]{2,1,0:T(1,128)S(1)}, u32[]{:S(2)}, u32[]{:S(2)}) %all-to-all-start) | async-done | bytes 524320 | tf_op jit(solution)/shard_map/all_to_all | solution.py:36
  53.6 0.5 broadcast.381
  54.1 1.9 reduce.1
  56.0 16.0 %reshape.806 = f32[4096,2,2,8]{3,2,1,0:T(2,128)} reshape(f32[8,16384]{1,0:T(8,128)S(1)} %reduce.1) | data formatting | bytes 1048576
  72.1 10.1 %copy.158 = f32[2,2,8,8,512]{4,2,1,3,0:T(8,128)S(1)} copy(f32[2,2,8,8,512]{2,1,0,4,3:T(2,128)} %bitcast.618) | data formatting | bytes 1048576 | tf_op jit(solution)/shard_map/all_to_all | solution.py:36
  82.3 0.0 copy-start.1
  82.4 0.0 copy-start.2
  82.4 0.0 copy-start.3
  82.4 0.0 copy-start.4
  82.4 0.0 copy-start.5
  82.4 0.0 copy-start.6
  82.4 0.0 copy-start.7
  82.4 0.0 copy-start.8
  82.4 0.0 copy-start.9
  82.4 0.0 copy-start.10
  82.4 0.0 copy-start.11
  82.5 0.4 fusion.51
  82.9 0.1 fusion.91
  83.0 0.1 fusion.92
  83.1 1.4 collective-permute-start.1
  84.5 4.5 %collective-permute-start.2 = (f32[16,8,1]{2,1,0:T(8,128)S(1)}, f32[16,8,1]{2,1,0:T(8,128)S(1)}, u32[]{:S(2)}, u32[]{:S(2)}) collective-permute-start(f32[16,8,1]{2,1,0:T(8,128)S(1)} %get-tuple-element.60), channel_id=1, source_target_pairs={{0,1},{1,2},{2,3},{3,4},{4,5},{5,6},{6,7},{8,9},{9,10},{10,11},{11... | collective-permute-start | bytes 1544 | tf_op jit(solution)/shard_map/ppermute | solution.py:18
  89.1 3.6 %collective-permute-start.3 = (f32[16,1,512]{2,1,0:T(1,128)S(1)}, f32[16,1,512]{2,1,0:T(1,128)S(1)}, u32[]{:S(2)}, u32[]{:S(2)}) collective-permute-start(f32[16,1,512]{2,1,0:T(1,128)S(1)} %get-tuple-element.57), channel_id=1, source_target_pairs={{8,0},{16,8},{24,16},{32,24},{40,32},{48,40},{56,48},{64,56},{72,6... | collective-permute-start | bytes 98312 | tf_op jit(solution)/shard_map/ppermute | solution.py:18
  92.7 1.9 collective-permute-start.4
  94.9 1.2 multiply_reduce_fusion.3
  96.1 0.1 fusion.93
  96.2 0.0 collective-permute-done.1
  96.2 0.0 collective-permute-done.2
  96.2 0.0 collective-permute-done.3
  96.2 5.1 %collective-permute-done.4 = f32[16,1,512]{2,1,0:T(1,128)S(1)} collective-permute-done((f32[16,1,512]{2,1,0:T(1,128)S(1)}, f32[16,1,512]{2,1,0:T(1,128)S(1)}, u32[]{:S(2)}, u32[]{:S(2)}) %collective-permute-start.4) | collective-permute-done | bytes 32800 | tf_op jit(solution)/shard_map/ppermute | solution.py:18
  101.3 0.3 fusion.2
  101.7 0.4 fusion.52
  102.1 0.1 fusion.86
  102.2 0.1 fusion.87
  102.4 1.3 collective-permute-start.5
  103.7 4.5 %collective-permute-start.6 = (f32[16,8,1]{2,1,0:T(8,128)S(1)}, f32[16,8,1]{2,1,0:T(8,128)S(1)}, u32[]{:S(2)}, u32[]{:S(2)}) collective-permute-start(f32[16,8,1]{2,1,0:T(8,128)S(1)} %get-tuple-element.35), channel_id=1, source_target_pairs={{0,1},{1,2},{2,3},{3,4},{4,5},{5,6},{6,7},{8,9},{9,10},{10,11},{11... | collective-permute-start | bytes 1544 | tf_op jit(solution)/shard_map/ppermute | solution.py:18
  108.2 1.9 collective-permute-start.7
  110.2 2.6 collective-permute-start.8
  112.8 0.1 fusion.88
  112.9 0.0 collective-permute-done.5
  112.9 0.0 collective-permute-done.6
  112.9 0.0 collective-permute-done.7
  112.9 5.8 %collective-permute-done.8 = f32[16,1,512]{2,1,0:T(1,128)S(1)} collective-permute-done((f32[16,1,512]{2,1,0:T(1,128)S(1)}, f32[16,1,512]{2,1,0:T(1,128)S(1)}, u32[]{:S(2)}, u32[]{:S(2)}) %collective-permute-start.8) | collective-permute-done | bytes 32800 | tf_op jit(solution)/shard_map/ppermute | solution.py:18
  118.8 1.5 multiply_reduce_fusion.2
  120.2 2.6 pad_maximum_fusion.5
  122.8 14.4 %psum.14 = f32[4]{0:T(128)S(1)} all-reduce(f32[4]{0:T(128)S(1)} %pad_maximum_fusion.5), channel_id=1, replica_groups=mesh['rows'=64,'dates'=8] {'dates'}, use_global_device_ids=true, to_apply=%region_4.5 | all-reduce | flops 4 | bytes 32 | tf_op jit(solution)/shard_map/psum | solution.py:11
  137.2 124.0 %psum.15 = f32[4]{0:T(128)S(1)} all-reduce(f32[4]{0:T(128)S(1)} %psum.14), channel_id=1, replica_groups=mesh['rows'=64,'dates'=8] {'rows'}, use_global_device_ids=true, to_apply=%region_5.6 | all-reduce | flops 4 | bytes 32 | tf_op jit(solution)/shard_map/psum | solution.py:11
  261.3 0.6 fusion.94
  268.2 1.6 fusion.19
  269.7 0.1 add_bitcast_fusion
  269.9 21.6 %all_to_all.30 = f32[2,16,8,512]{3,2,0,1:T(8,128)S(1)} all-to-all(f32[2,16,8,512]{3,2,0,1:T(8,128)S(1)} %pad_maximum_fusion.1), channel_id=1, replica_groups=mesh['rows'=64,'dates'=8] {'dates'}, dimensions={1} | all-to-all | bytes 1048576 | tf_op jit(solution)/shard_map/all_to_all | solution.py:94
  291.5 0.7 copy.176
  292.2 0.7 copy.177
  (68 shorter events, 0.5 us)
Async XLA Ops:
  10.0 26.1 %copy-start.23 = (s32[2,8,4096]{2,1,0:T(8,128)S(1)}, s32[2,8,4096]{2,1,0:T(8,128)}, u32[]{:S(2)}) copy-start(s32[2,8,4096]{2,1,0:T(8,128)} %param.9) | copy-start | bytes 786436
  25.7 13.4 %copy-start = (bf16[16,16,8,512]{3,2,1,0:T(8,128)(2,1)S(1)}, bf16[16,16,8,512]{3,2,1,0:T(8,128)(2,1)}, u32[]{:S(2)}) copy-start(bf16[16,16,8,512]{3,2,1,0:T(8,128)(2,1)} %param.11) | copy-start | bytes 6291460
  25.7 27.9 %all-to-all-start = ((f32[8,1,16384]{2,1,0:T(1,128)}), f32[8,1,16384]{2,1,0:T(1,128)S(1)}, u32[]{:S(2)}, u32[]{:S(2)}) async-start(f32[8,1,16384]{2,1,0:T(1,128)} %reshape.805), calls=%async_computation | async-start | bytes 1048576 | tf_op jit(solution)/shard_map/all_to_all | solution.py:36
  36.3 8.2 %collective-permute-start = (f32[1,512]{1,0:T(1,128)S(1)}, f32[1,512]{1,0:T(1,128)S(1)}, u32[]{:S(2)}, u32[]{:S(2)}) collective-permute-start(f32[1,512]{1,0:T(1,128)S(1)} %slice.360), channel_id=1, source_target_pairs={{0,8},{8,16},{16,24},{24,32},{32,40},{40,48},{48,56},{56,64},{64,7... | collective-permute-start | bytes 6152 | tf_op jit(solution)/shard_map/ppermute | solution.py:18
  39.1 1.9 copy-start.32
  82.3 36.5 %copy-start.16 = (f32[8,512]{1,0:T(8,128)}, f32[8,512]{1,0:T(8,128)S(1)}, u32[]{:S(2)}) copy-start(f32[8,512]{1,0:T(8,128)S(1)} %get-tuple-element.73) | copy-start | bytes 49156
  82.3 36.4 %copy-start.17 = (f32[8,512]{1,0:T(8,128)}, f32[8,512]{1,0:T(8,128)S(1)}, u32[]{:S(2)}) copy-start(f32[8,512]{1,0:T(8,128)S(1)} %get-tuple-element.74) | copy-start | bytes 49156
  82.3 36.4 %copy-start.18 = (f32[8,512]{1,0:T(8,128)}, f32[8,512]{1,0:T(8,128)S(1)}, u32[]{:S(2)}) copy-start(f32[8,512]{1,0:T(8,128)S(1)} %get-tuple-element.75) | copy-start | bytes 49156
  82.3 36.4 %copy-start.19 = (f32[8,512]{1,0:T(8,128)}, f32[8,512]{1,0:T(8,128)S(1)}, u32[]{:S(2)}) copy-start(f32[8,512]{1,0:T(8,128)S(1)} %get-tuple-element.76) | copy-start | bytes 49156
  82.3 36.4 %copy-start.20 = (f32[8,512]{1,0:T(8,128)}, f32[8,512]{1,0:T(8,128)S(1)}, u32[]{:S(2)}) copy-start(f32[8,512]{1,0:T(8,128)S(1)} %get-tuple-element.77) | copy-start | bytes 49156
  82.3 36.4 %copy-start.21 = (f32[8,512]{1,0:T(8,128)}, f32[8,512]{1,0:T(8,128)S(1)}, u32[]{:S(2)}) copy-start(f32[8,512]{1,0:T(8,128)S(1)} %get-tuple-element.78) | copy-start | bytes 49156
  82.3 36.4 %copy-start.22 = (f32[8,512]{1,0:T(8,128)}, f32[8,512]{1,0:T(8,128)S(1)}, u32[]{:S(2)}) copy-start(f32[8,512]{1,0:T(8,128)S(1)} %get-tuple-element.79) | copy-start | bytes 49156
  82.3 12.3 %copy-start.1 = (f32[16,1,8,512]{3,2,0,1:T(8,128)S(1)}, f32[16,1,8,512]{3,2,0,1:T(8,128)}, u32[]{:S(2)}) copy-start(f32[16,1,8,512]{3,2,0,1:T(8,128)} %get-tuple-element.11) | copy-start | bytes 786436
  82.4 12.3 %copy-start.2 = (f32[16,1,8,512]{3,2,0,1:T(8,128)S(1)}, f32[16,1,8,512]{3,2,0,1:T(8,128)}, u32[]{:S(2)}) copy-start(f32[16,1,8,512]{3,2,0,1:T(8,128)} %get-tuple-element.12) | copy-start | bytes 786436
  82.4 12.3 %copy-start.3 = (f32[16,1,8,512]{3,2,0,1:T(8,128)S(1)}, f32[16,1,8,512]{3,2,0,1:T(8,128)}, u32[]{:S(2)}) copy-start(f32[16,1,8,512]{3,2,0,1:T(8,128)} %get-tuple-element.13) | copy-start | bytes 786436
  82.4 12.3 %copy-start.4 = (f32[16,1,8,512]{3,2,0,1:T(8,128)S(1)}, f32[16,1,8,512]{3,2,0,1:T(8,128)}, u32[]{:S(2)}) copy-start(f32[16,1,8,512]{3,2,0,1:T(8,128)} %get-tuple-element.14) | copy-start | bytes 786436
  82.4 12.3 %copy-start.5 = (f32[16,1,8,512]{3,2,0,1:T(8,128)S(1)}, f32[16,1,8,512]{3,2,0,1:T(8,128)}, u32[]{:S(2)}) copy-start(f32[16,1,8,512]{3,2,0,1:T(8,128)} %get-tuple-element.15) | copy-start | bytes 786436
  82.4 12.3 %copy-start.6 = (f32[16,1,8,512]{3,2,0,1:T(8,128)S(1)}, f32[16,1,8,512]{3,2,0,1:T(8,128)}, u32[]{:S(2)}) copy-start(f32[16,1,8,512]{3,2,0,1:T(8,128)} %get-tuple-element.16) | copy-start | bytes 786436
  82.4 12.3 %copy-start.7 = (f32[16,1,8,512]{3,2,0,1:T(8,128)S(1)}, f32[16,1,8,512]{3,2,0,1:T(8,128)}, u32[]{:S(2)}) copy-start(f32[16,1,8,512]{3,2,0,1:T(8,128)} %get-tuple-element.17) | copy-start | bytes 786436
  82.4 12.3 %copy-start.8 = (f32[16,1,8,512]{3,2,0,1:T(8,128)S(1)}, f32[16,1,8,512]{3,2,0,1:T(8,128)}, u32[]{:S(2)}) copy-start(f32[16,1,8,512]{3,2,0,1:T(8,128)} %get-tuple-element.18) | copy-start | bytes 786436
  82.4 12.3 %copy-start.9 = (f32[16,1,8,512]{3,2,0,1:T(8,128)S(1)}, f32[16,1,8,512]{3,2,0,1:T(8,128)}, u32[]{:S(2)}) copy-start(f32[16,1,8,512]{3,2,0,1:T(8,128)} %get-tuple-element.19) | copy-start | bytes 786436
  82.4 12.3 %copy-start.10 = (f32[16,1,8,512]{3,2,0,1:T(8,128)S(1)}, f32[16,1,8,512]{3,2,0,1:T(8,128)}, u32[]{:S(2)}) copy-start(f32[16,1,8,512]{3,2,0,1:T(8,128)} %get-tuple-element.20) | copy-start | bytes 786436
  82.4 12.3 %copy-start.11 = (f32[16,1,8,512]{3,2,0,1:T(8,128)S(1)}, f32[16,1,8,512]{3,2,0,1:T(8,128)}, u32[]{:S(2)}) copy-start(f32[16,1,8,512]{3,2,0,1:T(8,128)} %get-tuple-element.21) | copy-start | bytes 786436
  82.5 12.3 %copy-start.12 = (f32[16,1,8,512]{3,2,0,1:T(8,128)S(1)}, f32[16,1,8,512]{3,2,0,1:T(8,128)}, u32[]{:S(2)}) copy-start(f32[16,1,8,512]{3,2,0,1:T(8,128)} %get-tuple-element.22) | copy-start | bytes 786436
  82.5 12.3 %copy-start.13 = (f32[16,1,8,512]{3,2,0,1:T(8,128)S(1)}, f32[16,1,8,512]{3,2,0,1:T(8,128)}, u32[]{:S(2)}) copy-start(f32[16,1,8,512]{3,2,0,1:T(8,128)} %get-tuple-element.23) | copy-start | bytes 786436
  82.5 12.3 %copy-start.14 = (f32[16,1,8,512]{3,2,0,1:T(8,128)S(1)}, f32[16,1,8,512]{3,2,0,1:T(8,128)}, u32[]{:S(2)}) copy-start(f32[16,1,8,512]{3,2,0,1:T(8,128)} %get-tuple-element.24) | copy-start | bytes 786436
  82.5 12.3 %copy-start.15 = (f32[16,1,8,512]{3,2,0,1:T(8,128)S(1)}, f32[16,1,8,512]{3,2,0,1:T(8,128)}, u32[]{:S(2)}) copy-start(f32[16,1,8,512]{3,2,0,1:T(8,128)} %get-tuple-element.25) | copy-start | bytes 786436
  83.1 13.1 %collective-permute-start.1 = (f32[16,8,1]{2,1,0:T(8,128)S(1)}, f32[16,8,1]{2,1,0:T(8,128)S(1)}, u32[]{:S(2)}, u32[]{:S(2)}) collective-permute-start(f32[16,8,1]{2,1,0:T(8,128)S(1)} %get-tuple-element.61), channel_id=1, source_target_pairs={{1,0},{2,1},{3,2},{4,3},{5,4},{6,5},{7,6},{9,8},{10,9},{11,10},{12... | collective-permute-start | bytes 1544 | tf_op jit(solution)/shard_map/ppermute | solution.py:18
  84.5 11.7 %collective-permute-start.2 = (f32[16,8,1]{2,1,0:T(8,128)S(1)}, f32[16,8,1]{2,1,0:T(8,128)S(1)}, u32[]{:S(2)}, u32[]{:S(2)}) collective-permute-start(f32[16,8,1]{2,1,0:T(8,128)S(1)} %get-tuple-element.60), channel_id=1, source_target_pairs={{0,1},{1,2},{2,3},{3,4},{4,5},{5,6},{6,7},{8,9},{9,10},{10,11},{11... | collective-permute-start | bytes 1544 | tf_op jit(solution)/shard_map/ppermute | solution.py:18
  89.1 7.1 %collective-permute-start.3 = (f32[16,1,512]{2,1,0:T(1,128)S(1)}, f32[16,1,512]{2,1,0:T(1,128)S(1)}, u32[]{:S(2)}, u32[]{:S(2)}) collective-permute-start(f32[16,1,512]{2,1,0:T(1,128)S(1)} %get-tuple-element.57), channel_id=1, source_target_pairs={{8,0},{16,8},{24,16},{32,24},{40,32},{48,40},{56,48},{64,56},{72,6... | collective-permute-start | bytes 98312 | tf_op jit(solution)/shard_map/ppermute | solution.py:18
  92.7 8.6 %collective-permute-start.4 = (f32[16,1,512]{2,1,0:T(1,128)S(1)}, f32[16,1,512]{2,1,0:T(1,128)S(1)}, u32[]{:S(2)}, u32[]{:S(2)}) collective-permute-start(f32[16,1,512]{2,1,0:T(1,128)S(1)} %get-tuple-element.56), channel_id=1, source_target_pairs={{0,8},{8,16},{16,24},{24,32},{32,40},{40,48},{48,56},{56,64},{64,7... | collective-permute-start | bytes 98312 | tf_op jit(solution)/shard_map/ppermute | solution.py:18
  94.8 6.5 %copy-start.24 = (f32[8,512]{1,0:T(8,128)S(1)}, f32[8,512]{1,0:T(8,128)}, u32[]{:S(2)}) copy-start(f32[8,512]{1,0:T(8,128)} %select_bitcast_fusion) | copy-start | bytes 49156
  94.8 6.5 %copy-start.25 = (f32[8,512]{1,0:T(8,128)S(1)}, f32[8,512]{1,0:T(8,128)}, u32[]{:S(2)}) copy-start(f32[8,512]{1,0:T(8,128)} %get-tuple-element.6) | copy-start | bytes 49156
  94.8 6.5 %copy-start.26 = (f32[8,512]{1,0:T(8,128)S(1)}, f32[8,512]{1,0:T(8,128)}, u32[]{:S(2)}) copy-start(f32[8,512]{1,0:T(8,128)} %get-tuple-element.7) | copy-start | bytes 49156
  94.8 6.5 %copy-start.27 = (f32[8,512]{1,0:T(8,128)S(1)}, f32[8,512]{1,0:T(8,128)}, u32[]{:S(2)}) copy-start(f32[8,512]{1,0:T(8,128)} %get-tuple-element.8) | copy-start | bytes 49156
  94.8 6.5 %copy-start.28 = (f32[8,512]{1,0:T(8,128)S(1)}, f32[8,512]{1,0:T(8,128)}, u32[]{:S(2)}) copy-start(f32[8,512]{1,0:T(8,128)} %get-tuple-element.9) | copy-start | bytes 49156
  94.8 6.5 %copy-start.29 = (f32[16]{0:T(128)S(1)}, f32[16]{0:T(128)}, u32[]{:S(2)}) copy-start(f32[16]{0:T(128)} %get-tuple-element.84) | copy-start | bytes 196
  94.9 6.5 %copy-start.30 = (f32[16]{0:T(128)S(1)}, f32[16]{0:T(128)}, u32[]{:S(2)}) copy-start(f32[16]{0:T(128)} %get-tuple-element.85) | copy-start | bytes 196
  94.9 6.5 %copy-start.31 = (f32[16]{0:T(128)S(1)}, f32[16]{0:T(128)}, u32[]{:S(2)}) copy-start(f32[16]{0:T(128)} %get-tuple-element.86) | copy-start | bytes 196
  102.4 10.5 %collective-permute-start.5 = (f32[16,8,1]{2,1,0:T(8,128)S(1)}, f32[16,8,1]{2,1,0:T(8,128)S(1)}, u32[]{:S(2)}, u32[]{:S(2)}) collective-permute-start(f32[16,8,1]{2,1,0:T(8,128)S(1)} %get-tuple-element.34), channel_id=1, source_target_pairs={{1,0},{2,1},{3,2},{4,3},{5,4},{6,5},{7,6},{9,8},{10,9},{11,10},{12... | collective-permute-start | bytes 1544 | tf_op jit(solution)/shard_map/ppermute | solution.py:18
  103.7 9.2 %collective-permute-start.6 = (f32[16,8,1]{2,1,0:T(8,128)S(1)}, f32[16,8,1]{2,1,0:T(8,128)S(1)}, u32[]{:S(2)}, u32[]{:S(2)}) collective-permute-start(f32[16,8,1]{2,1,0:T(8,128)S(1)} %get-tuple-element.35), channel_id=1, source_target_pairs={{0,1},{1,2},{2,3},{3,4},{4,5},{5,6},{6,7},{8,9},{9,10},{10,11},{11... | collective-permute-start | bytes 1544 | tf_op jit(solution)/shard_map/ppermute | solution.py:18
  108.2 4.6 %collective-permute-start.7 = (f32[16,1,512]{2,1,0:T(1,128)S(1)}, f32[16,1,512]{2,1,0:T(1,128)S(1)}, u32[]{:S(2)}, u32[]{:S(2)}) collective-permute-start(f32[16,1,512]{2,1,0:T(1,128)S(1)} %get-tuple-element.38), channel_id=1, source_target_pairs={{8,0},{16,8},{24,16},{32,24},{40,32},{48,40},{56,48},{64,56},{72,6... | collective-permute-start | bytes 98312 | tf_op jit(solution)/shard_map/ppermute | solution.py:18
  110.2 8.6 %collective-permute-start.8 = (f32[16,1,512]{2,1,0:T(1,128)S(1)}, f32[16,1,512]{2,1,0:T(1,128)S(1)}, u32[]{:S(2)}, u32[]{:S(2)}) collective-permute-start(f32[16,1,512]{2,1,0:T(1,128)S(1)} %get-tuple-element.39), channel_id=1, source_target_pairs={{0,8},{8,16},{16,24},{24,32},{32,40},{40,48},{48,56},{56,64},{64,7... | collective-permute-start | bytes 98312 | tf_op jit(solution)/shard_map/ppermute | solution.py:18
